TPU v7x, 32 devices: a whole 2x2x4 slice. The times are simulated.
32 devices in a mesh: gx: 2 (over core), gy: 4 (over y, x), gz: 4 (over z).
Axes of the slice: x: 2, y: 2, z: 4, core: 2. Of those that a mesh axis runs over, the one named last changes fastest.
Arguments:
- student: bfloat16 [1024, 1024], P('gx', 'gz'), may hold values from -12 to 12
- teacher: bfloat16 [8192, 1024], P('gy', 'gz'), may hold values from -6 to 6
- block_ids: int32 [8, 32], P('gx'), may hold values from 0 to 63, as said below
- block_valid: int32 [8, 32], P('gx'), may hold values from 0 to 1
Outputs:
- row_potential: float32 [1024], P('gx')
- column_potential: float32 [8192], P('gy')
Inputs may be any that keep to these rules, and one draw needn't show every extreme that they name: `block_ids`: within each row block the valid slots name distinct column blocks, and at most 8 of them lie in one aligned group of 16 column blocks; in every draw some row block has exactly 8 valid slots in one group.
All inputs are finite; a program needn't handle non-finite values.
Results may differ from a plain program's by a relative error of at most 0.0003.
Values sent between devices are 32-bit elements; how exact they have to be, the bound alone decides.
A program may use at most 64 MiB of HBM per device.

v0:
```python
import math

import jax
import jax.numpy as jnp
from jax import lax
from jax.sharding import PartitionSpec as P

F = 1024
TILE = 128
LOCAL_MOST = 8
ITERS = 5


SOFTNESS = 0.1
EXACT = lax.Precision.HIGHEST


def combined_all(x, axis, combine):
    everything = jax.tree.map(lambda part: lax.all_gather(part, axis), x)
    initial = jax.tree.map(lambda part: part[0], everything)

    def lap(k, so_far):
        return combine(so_far, jax.tree.map(lambda part: part[k], everything))

    return lax.fori_loop(1, lax.axis_size(axis), lap, initial)


def soft_bound(highest, totals):
    return -SOFTNESS * (highest + jnp.log(totals + jnp.exp(-highest)))


def pair_merge(earlier, later):
    highest = jnp.maximum(earlier[0], later[0])
    return (
        highest,
        earlier[1] * jnp.exp(earlier[0] - highest) + later[1] * jnp.exp(later[0] - highest),
    )


def row_partial(costs, column_values, one_hot, live_mask):
    gathered = jnp.einsum("rmb,bw->rmw", one_hot, column_values, precision=EXACT)
    scores = (gathered[:, :, :, None] - costs) / SOFTNESS
    highest = jnp.maximum(jnp.max(jnp.where(live_mask, scores, -1e30), axis=(1, 2)), 0.0)
    totals = jnp.sum(
        jnp.where(live_mask, jnp.exp(scores - highest[:, None, None, :]), 0.0), axis=(1, 2)
    )
    return (highest, totals)


def local_totals(scores, highest, one_hot, live_mask):
    chosen_peak = jnp.einsum("rmb,bw->rmw", one_hot, highest, precision=EXACT)
    tile_sum = jnp.sum(
        jnp.where(live_mask, jnp.exp(scores - chosen_peak[:, :, :, None]), 0.0), axis=3
    )
    return jnp.einsum("rmb,rmw->bw", one_hot, tile_sum, precision=EXACT)


def column_update(costs, row_values, one_hot, live_mask):
    scores = (row_values[:, None, None, :] - costs) / SOFTNESS
    tile_peak = jnp.max(scores, axis=3)
    spread_peak = jnp.where(one_hot[:, :, :, None] > 0, tile_peak[:, :, None, :], 0.0)
    local_peak = jnp.maximum(jnp.max(spread_peak, axis=(0, 1)), 0.0)
    partial_sum = local_totals(scores, local_peak, one_hot, live_mask)
    highest, totals = combined_all((local_peak, partial_sum), "gx", pair_merge)
    return soft_bound(highest, totals)


def on_device(student, teacher, block_ids, block_valid):
    span_blocks = teacher.shape[0] // TILE
    width_part = student.shape[1]
    column_index = lax.axis_index("gy")
    local_ids = block_ids - column_index * span_blocks
    owned = (block_valid > 0) & (local_ids >= 0) & (local_ids < span_blocks)
    slot_rank = jnp.cumsum(owned.astype(jnp.int32), axis=1) - 1
    slot_range = jnp.arange(LOCAL_MOST, dtype=jnp.int32)
    chosen_slots = (
        owned[:, None, :] & (slot_rank[:, None, :] == slot_range[None, :, None])
    ).astype(jnp.int32)
    live_slots = jnp.sum(chosen_slots, axis=2)
    block_of = jnp.sum(chosen_slots * local_ids[:, None, :], axis=2)
    block_range = jnp.arange(span_blocks, dtype=jnp.int32)
    one_hot = (
        (block_of[:, :, None] == block_range[None, None, :]) & (live_slots[:, :, None] > 0)
    ).astype(jnp.float32)
    live_mask = (live_slots > 0)[:, :, None, None]
    teacher_blocks = teacher.reshape(span_blocks, TILE, width_part)
    student_blocks = student.reshape(-1, TILE, width_part)
    picked = teacher_blocks[block_of]
    partial_dots = jnp.einsum(
        "rmcf,rif->rmci", picked, student_blocks, preferred_element_type=jnp.float32
    )
    cost_scale = -1.0 / math.sqrt(F)
    costs = lax.psum(partial_dots, "gz") * cost_scale
    column_values = jnp.zeros((span_blocks, costs.shape[2]), jnp.float32)
    row_values = jnp.zeros((student_blocks.shape[0], TILE), jnp.float32)
    for sweep in range(ITERS):
        highest, totals = row_partial(costs, column_values, one_hot, live_mask)
        highest, totals = combined_all((highest, totals), "gy", pair_merge)
        row_values = soft_bound(highest, totals)
        column_values = column_update(costs, row_values, one_hot, live_mask)
    return (row_values.reshape(-1), column_values.reshape(-1))


def solution(mesh):
    placed = (P("gx", "gz"), P("gy", "gz"), P("gx", None), P("gx", None))
    return jax.shard_map(
        on_device, mesh=mesh, in_specs=placed, out_specs=(P("gx"), P("gy")), check_vma=False
    )
```

profile of v0, /device:TPU:0, one launch (start us, length us, event | category | flops | bytes accessed | tf_op | source)
XLA Modules:
  0.0 226.9 jit_solution(7999439772396991120)
XLA Ops:
  7.2 0.8 fusion.164
  8.0 0.2 reduce_window_sum.11
  8.2 0.2 convert_reduce_fusion
  8.6 0.7 gather_fusion
  9.3 0.3 copy-done.2
  9.5 2.0 fusion.165
  11.6 0.2 fusion.40
  11.8 88.7 %all-reduce.2.cloned.1.call-done = f32[4,8,128,128]{3,2,1,0:T(8,128)} async-done(((f32[4,8,128,128]{3,2,1,0:T(8,128)}), f32[4,8,128,128]{3,2,1,0:T(8,128)}) %all-reduce.2.cloned.1.call-update) | async-done | bytes 2097168 | tf_op jit(solution)/shard_map/psum | solution.py:93
  100.6 2.1 select_reduce_fusion.14
  102.8 0.8 select_reduce_fusion.13
  103.6 8.1 %all-gather.21 = f32[4,4,128]{2,1,0:T(4,128)S(1)} all-gather(f32[1,4,128]{2,1,0:T(4,128)S(1)} %bitcast.193), channel_id=3, replica_groups=mesh['gx'=2,'gy'=4,'gz'=4] {'gy'}, dimensions={0}, use_global_device_ids=true | all-gather | bytes 10240 | tf_op jit(solution)/shard_map/all_gather | solution.py:19
  111.6 8.0 %all-gather.20 = f32[4,4,128]{2,1,0:T(4,128)S(1)} all-gather(f32[1,4,128]{2,1,0:T(4,128)S(1)} %get-tuple-element.841), channel_id=2, replica_groups=mesh['gx'=2,'gy'=4,'gz'=4] {'gy'}, dimensions={0}, use_global_device_ids=true | all-gather | bytes 10240 | tf_op jit(solution)/shard_map/all_gather | solution.py:19
  119.8 0.6 fusion.10
  120.6 0.2 fusion.38
  120.8 1.3 select_reduce_fusion.12
  122.1 0.3 convolution_bitcast_fusion.4
  122.4 1.8 all-gather.3
  124.2 1.8 all-gather.2
  126.0 0.2 fusion.35
  126.2 0.8 select_reduce_fusion.11
  127.0 0.8 select_reduce_fusion.10
  127.8 7.1 %all-gather.23 = f32[4,4,128]{2,1,0:T(4,128)S(1)} all-gather(f32[1,4,128]{2,1,0:T(4,128)S(1)} %bitcast.194), channel_id=7, replica_groups=mesh['gx'=2,'gy'=4,'gz'=4] {'gy'}, dimensions={0}, use_global_device_ids=true | all-gather | bytes 10240 | tf_op jit(solution)/shard_map/all_gather | solution.py:19
  134.9 8.0 %all-gather.22 = f32[4,4,128]{2,1,0:T(4,128)S(1)} all-gather(f32[1,4,128]{2,1,0:T(4,128)S(1)} %get-tuple-element.839), channel_id=6, replica_groups=mesh['gx'=2,'gy'=4,'gz'=4] {'gy'}, dimensions={0}, use_global_device_ids=true | all-gather | bytes 10240 | tf_op jit(solution)/shard_map/all_gather | solution.py:19
  143.1 0.6 fusion.11
  143.7 0.1 select_reduce_fusion.18
  143.9 0.2 fusion.33
  144.1 1.3 select_reduce_fusion.9
  145.4 0.3 convolution_bitcast_fusion.3
  145.7 1.8 all-gather.7
  147.5 1.8 all-gather.6
  149.3 0.2 fusion.30
  149.5 0.8 select_reduce_fusion.8
  150.3 0.8 select_reduce_fusion.7
  151.1 7.1 %all-gather.25 = f32[4,4,128]{2,1,0:T(4,128)S(1)} all-gather(f32[1,4,128]{2,1,0:T(4,128)S(1)} %bitcast.195), channel_id=11, replica_groups=mesh['gx'=2,'gy'=4,'gz'=4] {'gy'}, dimensions={0}, use_global_device_ids=true | all-gather | bytes 10240 | tf_op jit(solution)/shard_map/all_gather | solution.py:19
  158.2 8.0 %all-gather.24 = f32[4,4,128]{2,1,0:T(4,128)S(1)} all-gather(f32[1,4,128]{2,1,0:T(4,128)S(1)} %get-tuple-element.837), channel_id=10, replica_groups=mesh['gx'=2,'gy'=4,'gz'=4] {'gy'}, dimensions={0}, use_global_device_ids=true | all-gather | bytes 10240 | tf_op jit(solution)/shard_map/all_gather | solution.py:19
  166.4 0.6 fusion.12
  167.2 0.2 fusion.28
  167.4 1.3 select_reduce_fusion.6
  168.7 0.3 convolution_bitcast_fusion.2
  169.0 1.8 all-gather.11
  170.8 1.8 all-gather.10
  172.6 0.2 fusion.25
  172.8 0.8 select_reduce_fusion.5
  173.6 0.8 select_reduce_fusion.4
  174.4 7.1 %all-gather.27 = f32[4,4,128]{2,1,0:T(4,128)S(1)} all-gather(f32[1,4,128]{2,1,0:T(4,128)S(1)} %bitcast.196), channel_id=15, replica_groups=mesh['gx'=2,'gy'=4,'gz'=4] {'gy'}, dimensions={0}, use_global_device_ids=true | all-gather | bytes 10240 | tf_op jit(solution)/shard_map/all_gather | solution.py:19
  181.5 8.0 %all-gather.26 = f32[4,4,128]{2,1,0:T(4,128)S(1)} all-gather(f32[1,4,128]{2,1,0:T(4,128)S(1)} %get-tuple-element.835), channel_id=14, replica_groups=mesh['gx'=2,'gy'=4,'gz'=4] {'gy'}, dimensions={0}, use_global_device_ids=true | all-gather | bytes 10240 | tf_op jit(solution)/shard_map/all_gather | solution.py:19
  189.7 0.6 fusion.13
  190.5 0.2 fusion.23
  190.7 1.3 select_reduce_fusion.3
  192.0 0.3 convolution_bitcast_fusion.1
  192.3 1.8 all-gather.15
  194.1 2.0 all-gather.14
  196.1 0.2 fusion.20
  196.3 0.8 select_reduce_fusion.2
  197.1 0.8 select_reduce_fusion.1
  197.8 7.1 %all-gather.29 = f32[4,4,128]{2,1,0:T(4,128)S(1)} all-gather(f32[1,4,128]{2,1,0:T(4,128)S(1)} %bitcast.197), channel_id=19, replica_groups=mesh['gx'=2,'gy'=4,'gz'=4] {'gy'}, dimensions={0}, use_global_device_ids=true | all-gather | bytes 10240 | tf_op jit(solution)/shard_map/all_gather | solution.py:19
  205.0 8.0 %all-gather.28 = f32[4,4,128]{2,1,0:T(4,128)S(1)} all-gather(f32[1,4,128]{2,1,0:T(4,128)S(1)} %get-tuple-element.833), channel_id=18, replica_groups=mesh['gx'=2,'gy'=4,'gz'=4] {'gy'}, dimensions={0}, use_global_device_ids=true | all-gather | bytes 10240 | tf_op jit(solution)/shard_map/all_gather | solution.py:19
  213.2 0.6 fusion.14
  213.9 0.2 fusion.18
  214.2 1.3 select_reduce_fusion
  215.5 0.3 convolution_bitcast_fusion
  215.8 1.8 all-gather.19
  217.6 1.8 all-gather.18
  219.4 0.6 fusion.47
  (64 shorter events, 2.0 us)
Async XLA Ops:
  7.2 1.4 copy-start
  7.2 93.4 %all-reduce.2.cloned.1.call-start = ((), (), s32[]{:S(2)}) async-start(), calls=%async_computation | async-start | bytes 4194304 | tf_op jit(solution)/shard_map/psum | solution.py:93
  8.6 1.0 copy-start.2
  100.6 2.2 copy-start.1
  213.2 2.3 %copy-start.3 = (f32[4,128]{1,0:T(4,128)}, f32[4,128]{1,0:T(4,128)S(1)}, u32[]{:S(2)}) copy-start(f32[4,128]{1,0:T(4,128)S(1)} %add_multiply_fusion) | copy-start | bytes 6148
Sparse Core Ops, SparseCore 0:
  11.7 88.8 all-reduce.1
where the time goes:
time: 227 us
  blocking collectives  95.1 us (42%)
  waiting for transfers between devices  88.8 us (39%)
  other arithmetic  22 us (10%)
  between operations  14.4 us (6%)
  matrix products  5.22 us (2%)
    all_gather x20, blocking collectives, combined_all(): everything = jax.tree.map(lambda part: lax.all_gather(part, axis), x)  95.1 us
    psum x1, waiting for transfers between devices, on_device(): costs = lax.psum(partial_dots, 'gz') * cost_scale  88.7 us
    reduce_sum x5, other arithmetic, local_totals(): jnp.sum(jnp.where(live_mask, jnp.exp(scores - chosen_peak[:, :, :, None])...  6.74 us
    reduce_max x5, other arithmetic, row_partial(): jnp.max(jnp.where(live_mask, scores, -1e+30), axis=(1, 2))  5.15 us
  transfers between devices with their start and end apart: 1, of which 1 were waited for; matrix products, arithmetic and copies ran while one was open for 0% of the time, Pallas kernels for 0%

commit v1 on v0

v1 whole, which is shorter than its diff:
```python
import functools
import math

import jax
import jax.numpy as jnp
from jax import lax
from jax.experimental import pallas as pl
from jax.experimental.pallas import tpu as pltpu
from jax.sharding import PartitionSpec as P

F = 1024
TILE = 128
ITERS = 5
SOFTNESS = 0.1
MESH = pl.DeviceIdType.MESH


def spread(values):
    return [
        jnp.broadcast_to(values[k : k + 1], (TILE, TILE)).T for k in range(values.shape[0])
    ]


def kernel(
    sizes, student, teacher, ids, valid, row_out, col_out,
    stu_stage, stu_buf, tea_stage, tea_buf, kern,
    first_send, first_recv, row_send, row_recv, col_send, col_recv, fin_recv,
    stu_ss, stu_rs, tea_ss, tea_rs, row_ss, row_rs, col_ss, col_rs,
):
    gx, gy, gz, chunks = sizes
    ix, iy, iz = lax.axis_index("gx"), lax.axis_index("gy"), lax.axis_index("gz")
    rows = student.shape[0]
    cols = teacher.shape[0] // gz
    row_blocks, col_blocks = rows // TILE, cols // TILE
    quarter = rows // gy
    part = cols // gx
    piece = part // chunks

    def peer(dx=0, dy=0, dz=0):
        return {
            "gx": lax.rem(ix + dx, gx),
            "gy": lax.rem(iy + dy, gy),
            "gz": lax.rem(iz + dz, gz),
        }

    def send(src, dst, send_sem, recv_sem, target):
        copy = pltpu.make_async_remote_copy(
            src_ref=src, dst_ref=dst, send_sem=send_sem, recv_sem=recv_sem,
            device_id=target, device_id_type=MESH,
        )
        copy.start()
        return copy

    row_peers = [(a, b) for a in range(gy) for b in range(gz) if a or b]
    end_peers = [(a, b) for a in range(gx) for b in range(gz) if a or b]
    barrier = pltpu.get_barrier_semaphore()
    greeted = [peer(dy=a, dz=b) for a, b in row_peers]
    greeted += [peer(dx=a, dz=b) for a, b in end_peers if a]
    for target in greeted:
        pl.semaphore_signal(barrier, inc=1, device_id=target, device_id_type=MESH)

    my_quarter = pl.ds(pl.multiple_of(iy * quarter, 8), quarter)
    stu_stage[...] = student[my_quarter, :].astype(jnp.float32)
    for d in range(1, gz):
        first = lax.rem(iz + d, gz) * cols + ix * part
        tea_stage[d - 1] = teacher[pl.ds(pl.multiple_of(first, 8), part), :].astype(jnp.float32)
    pl.semaphore_wait(barrier, len(greeted))

    order = sorted(range(1, gz), key=lambda d: min(d, gz - d))
    copies = []
    stu_first = {}
    for d in order[::-1]:
        stu_first[d] = send(
            stu_stage, stu_buf.at[d - 1, my_quarter], stu_ss.at[d - 1, 0],
            stu_rs.at[d - 1, 0], peer(dz=d),
        )
    tea_first = {}
    for c in range(chunks):
        for d in order[::-1]:
            here = pl.ds(c * piece, piece)
            there = pl.ds(pl.multiple_of(ix * part + c * piece, 8), piece)
            tea_first[d, c] = send(
                tea_stage.at[d - 1, here], tea_buf.at[d - 1, there],
                tea_ss.at[d - 1, 0, c], tea_rs.at[d - 1, 0, c], peer(dz=d),
            )
    copies += list(stu_first.values()) + list(tea_first.values())

    def product(a, b):
        return lax.dot_general(
            a, b, (((1,), (1,)), ((), ())), preferred_element_type=jnp.float32
        )

    mine = teacher[pl.ds(pl.multiple_of(iz * cols, 8), cols), :]
    kern[...] = product(student[...], mine)

    stu_second, tea_second = {}, {}
    for d in order:
        stu_first[d].wait_recv()
        block = stu_buf.at[d - 1, my_quarter]
        for e in range(1, gy):
            stu_second[d, e] = send(
                block, block, stu_ss.at[d - 1, e], stu_rs.at[d - 1, e], peer(dy=e)
            )
    for c in range(chunks):
        for d in order:
            tea_first[d, c].wait_recv()
            there = pl.ds(pl.multiple_of(ix * part + c * piece, 8), piece)
            block = tea_buf.at[d - 1, there]
            for e in range(1, gx):
                tea_second[d, c, e] = send(
                    block, block, tea_ss.at[d - 1, e, c], tea_rs.at[d - 1, e, c], peer(dx=e)
                )
    copies += list(stu_second.values()) + list(tea_second.values())
    for d in order:
        for e in range(1, gy):
            stu_second[d, e].wait_recv()
        for c in range(chunks):
            for e in range(1, gx):
                tea_second[d, c, e].wait_recv()
        kern[...] += product(
            stu_buf[d - 1].astype(jnp.bfloat16), tea_buf[d - 1].astype(jnp.bfloat16)
        )

    scale = 1.0 / (math.sqrt(F) * SOFTNESS)
    first_block = (iy * gz + iz) * col_blocks
    live_slot = valid[...] > 0
    hits = [
        jnp.max(jnp.where(live_slot & (ids[...] == first_block + c), 1.0, 0.0), axis=1, keepdims=True)
        for c in range(col_blocks)
    ]

    def tile(r, c):
        return pl.ds(r * TILE, TILE), pl.ds(c * TILE, TILE)

    peaks, sums = [], []
    for r in range(row_blocks):
        on = [jnp.broadcast_to(hits[c][r : r + 1], (TILE, TILE)) > 0 for c in range(col_blocks)]
        x = [kern[tile(r, c)] * scale for c in range(col_blocks)]
        top = functools.reduce(
            jnp.maximum, [jnp.where(on[c], x[c], 0.0) for c in range(col_blocks)]
        )
        peak = jnp.maximum(jnp.max(top.T, axis=0, keepdims=True), 0.0)
        base = spread(peak)[0]
        total = jnp.zeros((TILE, TILE), jnp.float32)
        for c in range(col_blocks):
            value = jnp.where(on[c], jnp.exp(jnp.minimum(x[c] - base, 0.0)), 0.0)
            kern[tile(r, c)] = value
            total += value
        peaks.append(peak)
        sums.append(jnp.sum(total.T, axis=0, keepdims=True))
    peak = jnp.concatenate(peaks, axis=0)
    total = jnp.concatenate(sums, axis=0)

    def exchange(src, dst, send_sem, recv_sem, targets):
        for k, target in enumerate(targets):
            send(src, dst.at[k], send_sem, recv_sem, target)
        pltpu.make_async_copy(dst, dst, recv_sem).wait()

    def sent(dst, send_sem):
        pltpu.make_async_copy(dst, dst, send_sem).wait()

    row_targets = [peer(dy=a, dz=b) for a, b in row_peers]
    col_targets = [peer(dx=a) for a in range(1, gx)]
    end_targets = [peer(dx=a, dz=b) for a, b in end_peers]

    first_send[0] = peak
    first_send[1] = total
    exchange(first_send, first_recv, row_ss.at[0], row_rs.at[0], row_targets)
    highest = functools.reduce(
        jnp.maximum, [first_recv[k, 0] for k in range(len(row_peers))], peak
    )
    totals = total * jnp.exp(peak - highest)
    for k in range(len(row_peers)):
        totals += first_recv[k, 1] * jnp.exp(first_recv[k, 0] - highest)
    level = highest + jnp.log(totals + jnp.exp(-highest))
    share = jnp.exp(peak - level)
    rest = jnp.exp(-level)
    row_total = None

    for t in range(ITERS):
        if t > 0:
            weights = 1.0 / (1.0 + col_total)
            parts = []
            for r in range(row_blocks):
                total = jnp.zeros((TILE, TILE), jnp.float32)
                for c in range(col_blocks):
                    total += kern[tile(r, c)] * weights[c : c + 1]
                parts.append(jnp.sum(total.T, axis=0, keepdims=True))
            own = jnp.concatenate(parts, axis=0) * share
            row_send[t - 1] = own
            exchange(
                row_send.at[t - 1], row_recv.at[t - 1], row_ss.at[t], row_rs.at[t], row_targets
            )
            row_total = rest + own
            for k in range(len(row_peers)):
                row_total += row_recv[t - 1, k]
            factors = spread(share / row_total)
        else:
            factors = spread(share)
        parts = []
        for c in range(col_blocks):
            total = jnp.zeros((TILE, TILE), jnp.float32)
            for r in range(row_blocks):
                total += kern[tile(r, c)] * factors[r]
            parts.append(jnp.sum(total, axis=0, keepdims=True))
        own = jnp.concatenate(parts, axis=0)
        col_send[t] = own
        if t < ITERS - 1:
            exchange(col_send.at[t], col_recv.at[t], col_ss.at[t], col_rs.at[t], col_targets)
            col_total = own
            for k in range(gx - 1):
                col_total += col_recv[t, k]
        else:
            exchange(col_send.at[t], fin_recv, col_ss.at[t], col_rs.at[t], end_targets)
            for b in range(gz):
                col_total = own if b == 0 else jnp.zeros_like(own)
                for k, (_, db) in enumerate(end_peers):
                    if db == b:
                        col_total += fin_recv[k]
                col_out[lax.rem(iz + gz - b, gz)] = -SOFTNESS * jnp.log(1.0 + col_total)
    row_out[...] = -SOFTNESS * (level + jnp.log(row_total))

    for copy in copies:
        copy.wait_send()
    sent(first_recv, row_ss.at[0])
    for t in range(1, ITERS):
        sent(row_recv.at[t - 1], row_ss.at[t])
        sent(col_recv.at[t - 1], col_ss.at[t - 1])
    sent(fin_recv, col_ss.at[ITERS - 1])


def solution(mesh):
    gx, gy, gz = (mesh.shape[axis] for axis in ("gx", "gy", "gz"))

    def on_device(student, teacher, block_ids, block_valid):
        rows, width = student.shape
        cols = teacher.shape[0] // gz
        row_blocks, col_blocks = rows // TILE, cols // TILE
        part = cols // gx
        chunks = max(1, min(4, part // 64))
        row_peers, end_peers = gy * gz - 1, gx * gz - 1
        f32 = jnp.float32
        dma = pltpu.SemaphoreType.DMA
        row, col = pl.pallas_call(
            functools.partial(kernel, (gx, gy, gz, chunks)),
            out_shape=(
                jax.ShapeDtypeStruct((row_blocks, TILE), f32),
                jax.ShapeDtypeStruct((gz, col_blocks, TILE), f32),
            ),
            in_specs=[pl.BlockSpec(memory_space=pltpu.VMEM)] * 4,
            out_specs=(pl.BlockSpec(memory_space=pltpu.VMEM),) * 2,
            scratch_shapes=[
                pltpu.VMEM((rows // gy, width), f32),
                pltpu.VMEM((gz - 1, rows, width), f32),
                pltpu.VMEM((gz - 1, part, width), f32),
                pltpu.VMEM((gz - 1, cols, width), f32),
                pltpu.VMEM((rows, cols), f32),
                pltpu.VMEM((2, row_blocks, TILE), f32),
                pltpu.VMEM((row_peers, 2, row_blocks, TILE), f32),
                pltpu.VMEM((ITERS - 1, row_blocks, TILE), f32),
                pltpu.VMEM((ITERS - 1, row_peers, row_blocks, TILE), f32),
                pltpu.VMEM((ITERS, col_blocks, TILE), f32),
                pltpu.VMEM((ITERS - 1, gx - 1, col_blocks, TILE), f32),
                pltpu.VMEM((end_peers, col_blocks, TILE), f32),
                dma((gz - 1, gy)),
                dma((gz - 1, gy)),
                dma((gz - 1, gx, chunks)),
                dma((gz - 1, gx, chunks)),
                dma((ITERS,)),
                dma((ITERS,)),
                dma((ITERS,)),
                dma((ITERS,)),
            ],
            compiler_params=pltpu.CompilerParams(collective_id=0, has_side_effects=True),
        )(student, teacher, block_ids, block_valid)
        return row.reshape(-1), col.reshape(-1)

    placed = (P("gx", "gz"), P("gy", "gz"), P("gx", None), P("gx", None))
    return jax.shard_map(
        on_device, mesh=mesh, in_specs=placed, out_specs=(P("gx"), P("gy")), check_vma=False
    )
```

time: 227 us -> 77.9 us (0.34)
  blocking collectives: 95.1 us -> 0 us
  waiting for transfers between devices: 88.8 us -> 0 us
  Pallas kernels: 0 us -> 75.2 us
  other arithmetic: 22 us -> 0 us
  between operations: 14.4 us -> 0.65 us
  matrix products: 5.22 us -> 0 us
    all_gather x20 -> x0, blocking collectives: 95.1 us -> none  [combined_all(): everything = jax.tree.map(lambda part: lax.all_gather(part, axis), x)]
    psum x1 -> x0, waiting for transfers between devices: 88.7 us -> none  [on_device(): costs = lax.psum(partial_dots, 'gz') * cost_scale]
    pallas_call x0 -> x1, Pallas kernels: none -> 75.2 us  [on_device(): pl.pallas_call(functools.partial(kernel, (gx, gy, gz, chunks)), out_shape...]
    reduce_sum x11 -> x0, other arithmetic: 10.8 us -> none  [the longest x5 6.74 us: local_totals(): jnp.sum(jnp.where(live_mask, jnp.exp(scores - chosen_peak[:, :, :, None])...]
    reduce_max x15 -> x0, other arithmetic: 8.92 us -> none  [the longest x5 5.15 us: row_partial(): jnp.max(jnp.where(live_mask, scores, -1e+30), axis=(1, 2))]
    dot_general x16 -> x0, matrix products: 5.22 us -> none  [the longest x1 2 us: on_device(): jnp.einsum('rmcf,rif->rmci', picked, student_blocks, preferred_element_ty...]
  transfers between devices with their start and end apart: 1 -> 0, of which waited for: 1 -> 0; matrix products, arithmetic and copies ran while one was open for 0% -> 0% of each run, Pallas kernels for 0% -> 0%
where the time goes in v1:
time: 77.9 us; the launch traced here: 77.7 us
  Pallas kernels  75.2 us (97%)
  local copies, waits for them, and re-layouts  1.85 us (2%)
    pallas_call x1, Pallas kernels, on_device(): pl.pallas_call(functools.partial(kernel, (gx, gy, gz, chunks)), out_shape...  75.2 us
    unnamed x4, local copies, waits for them, and re-layouts  1.85 us

profile of v1, /device:TPU:0, one launch (start us, length us, event | category | flops | bytes accessed | tf_op | source)
XLA Modules:
  0.0 77.7 jit_solution(14610939142226391583)
XLA Ops:
  0.6 75.2 %shard_map.59 = (f32[4,128]{1,0:T(4,128)}, f32[4,4,128]{2,1,0:T(4,128)}) custom-call(bf16[512,256]{1,0:T(8,128)(2,1)} %student.1, bf16[2048,256]{1,0:T(8,128)(2,1)} %teacher.1, s32[4,32]{1,0:T(4,128)} %ids.1, s32[4,32]{1,0:T(4,128)} %valid.1), custom_call_target="tpu_custom_call" | custom-call | tf_op jit(solution)/shard_map/pallas_call | solution.py:244
  75.9 0.0 copy-start
  75.9 1.3 %copy.8 = f32[512]{0:T(512)} copy(f32[512]{0:T(512)} %bitcast.3) | data formatting | bytes 4096
  77.1 0.0 copy-done
  77.1 0.6 copy.9
Async XLA Ops:
  75.9 1.3 %copy-start = (f32[4,4,128]{2,1,0:T(4,128)S(1)}, f32[4,4,128]{2,1,0:T(4,128)}, u32[]{:S(2)}) copy-start(f32[4,4,128]{2,1,0:T(4,128)} %get-tuple-element.5) | copy-start | bytes 24580

commit v2 on v1

--- a/solution.py
+++ b/solution.py
@@ -43,6 +43,17 @@
             "gz": lax.rem(iz + dz, gz),
         }
 
+    def across(d):
+        mirrored, step = 0, 1
+        while step < gz:
+            bit = lax.rem(lax.div(iz, step), 2)
+            mirrored += (1 - bit if d & step else bit) * step
+            step *= 2
+        return mirrored
+
+    def facing(d):
+        return {"gx": ix, "gy": iy, "gz": across(d)}
+
     def send(src, dst, send_sem, recv_sem, target):
         copy = pltpu.make_async_remote_copy(
             src_ref=src, dst_ref=dst, send_sem=send_sem, recv_sem=recv_sem,
@@ -62,17 +73,18 @@
     my_quarter = pl.ds(pl.multiple_of(iy * quarter, 8), quarter)
     stu_stage[...] = student[my_quarter, :].astype(jnp.float32)
     for d in range(1, gz):
-        first = lax.rem(iz + d, gz) * cols + ix * part
+        first = across(d) * cols + ix * part
         tea_stage[d - 1] = teacher[pl.ds(pl.multiple_of(first, 8), part), :].astype(jnp.float32)
     pl.semaphore_wait(barrier, len(greeted))
 
-    order = sorted(range(1, gz), key=lambda d: min(d, gz - d))
+    order = sorted(range(1, gz), key=lambda d: (bin(d).count("1"), -d))
+    bits = [d for d in order if d & (d - 1) == 0]
     copies = []
     stu_first = {}
-    for d in order[::-1]:
+    for d in bits:
         stu_first[d] = send(
             stu_stage, stu_buf.at[d - 1, my_quarter], stu_ss.at[d - 1, 0],
-            stu_rs.at[d - 1, 0], peer(dz=d),
+            stu_rs.at[d - 1, 0], facing(d),
         )
     tea_first = {}
     for c in range(chunks):
@@ -81,9 +93,8 @@
             there = pl.ds(pl.multiple_of(ix * part + c * piece, 8), piece)
             tea_first[d, c] = send(
                 tea_stage.at[d - 1, here], tea_buf.at[d - 1, there],
-                tea_ss.at[d - 1, 0, c], tea_rs.at[d - 1, 0, c], peer(dz=d),
+                tea_ss.at[d - 1, 0, c], tea_rs.at[d - 1, 0, c], facing(d),
             )
-    copies += list(stu_first.values()) + list(tea_first.values())
 
     def product(a, b):
         return lax.dot_general(
@@ -97,6 +108,13 @@
     for d in order:
         stu_first[d].wait_recv()
         block = stu_buf.at[d - 1, my_quarter]
+        for b in bits:
+            if b < (d & -d):
+                far = d | b
+                stu_first[far] = send(
+                    block, stu_buf.at[far - 1, my_quarter], stu_ss.at[far - 1, 0],
+                    stu_rs.at[far - 1, 0], facing(b),
+                )
         for e in range(1, gy):
             stu_second[d, e] = send(
                 block, block, stu_ss.at[d - 1, e], stu_rs.at[d - 1, e], peer(dy=e)
@@ -110,6 +128,7 @@
                 tea_second[d, c, e] = send(
                     block, block, tea_ss.at[d - 1, e, c], tea_rs.at[d - 1, e, c], peer(dx=e)
                 )
+    copies += list(stu_first.values()) + list(tea_first.values())
     copies += list(stu_second.values()) + list(tea_second.values())
     for d in order:
         for e in range(1, gy):
@@ -231,6 +250,7 @@
 
 def solution(mesh):
     gx, gy, gz = (mesh.shape[axis] for axis in ("gx", "gy", "gz"))
+    assert gz & (gz - 1) == 0
 
     def on_device(student, teacher, block_ids, block_valid):
         rows, width = student.shape

time: 77.9 us -> 76 us (0.976)
  Pallas kernels: 75.2 us -> 73.4 us
    pallas_call x1, Pallas kernels: 75.2 us -> 73.4 us  [on_device(): pl.pallas_call(functools.partial(kernel, (gx, gy, gz, chunks)), out_shape...]
where the time goes in v2:
time: 76 us; the launch traced here: 75.9 us
  Pallas kernels  73.4 us (97%)
  local copies, waits for them, and re-layouts  1.85 us (2%)
    pallas_call x1, Pallas kernels, on_device(): pl.pallas_call(functools.partial(kernel, (gx, gy, gz, chunks)), out_shape...  73.4 us
    unnamed x4, local copies, waits for them, and re-layouts  1.85 us

profile of v2, /device:TPU:0, one launch (start us, length us, event | category | flops | bytes accessed | tf_op | source)
XLA Modules:
  0.0 75.9 jit_solution(4733691162084124726)
XLA Ops:
  0.6 73.4 %shard_map.59 = (f32[4,128]{1,0:T(4,128)}, f32[4,4,128]{2,1,0:T(4,128)}) custom-call(bf16[512,256]{1,0:T(8,128)(2,1)} %student.1, bf16[2048,256]{1,0:T(8,128)(2,1)} %teacher.1, s32[4,32]{1,0:T(4,128)} %ids.1, s32[4,32]{1,0:T(4,128)} %valid.1), custom_call_target="tpu_custom_call" | custom-call | tf_op jit(solution)/shard_map/pallas_call | solution.py:264
  74.0 0.0 copy-start
  74.0 1.3 %copy.8 = f32[512]{0:T(512)} copy(f32[512]{0:T(512)} %bitcast.3) | data formatting | bytes 4096
  75.3 0.0 copy-done
  75.3 0.6 copy.9
Async XLA Ops:
  74.0 1.3 %copy-start = (f32[4,4,128]{2,1,0:T(4,128)S(1)}, f32[4,4,128]{2,1,0:T(4,128)}, u32[]{:S(2)}) copy-start(f32[4,4,128]{2,1,0:T(4,128)} %get-tuple-element.5) | copy-start | bytes 24580

commit v3 on v2

--- a/solution.py
+++ b/solution.py
@@ -87,7 +87,7 @@
             stu_rs.at[d - 1, 0], facing(d),
         )
     tea_first = {}
-    for c in range(chunks):
+    for c in range((chunks + 1) // 2):
         for d in order[::-1]:
             here = pl.ds(c * piece, piece)
             there = pl.ds(pl.multiple_of(ix * part + c * piece, 8), piece)
@@ -119,6 +119,15 @@
             stu_second[d, e] = send(
                 block, block, stu_ss.at[d - 1, e], stu_rs.at[d - 1, e], peer(dy=e)
             )
+    for c in range((chunks + 1) // 2, chunks):
+        for d in order[::-1]:
+            here = pl.ds(c * piece, piece)
+            there = pl.ds(pl.multiple_of(ix * part + c * piece, 8), piece)
+            tea_first[d, c] = send(
+                tea_stage.at[d - 1, here], tea_buf.at[d - 1, there],
+                tea_ss.at[d - 1, 0, c], tea_rs.at[d - 1, 0, c], facing(d),
+            )
+
     for c in range(chunks):
         for d in order:
             tea_first[d, c].wait_recv()

time: 76 us -> 72.8 us (0.958)
  Pallas kernels: 73.4 us -> 70.1 us
    pallas_call x1, Pallas kernels: 73.4 us -> 70.1 us  [on_device(): pl.pallas_call(functools.partial(kernel, (gx, gy, gz, chunks)), out_shape...]
where the time goes in v3:
time: 72.8 us; the launch traced here: 72.6 us
  Pallas kernels  70.1 us (96%)
  local copies, waits for them, and re-layouts  1.85 us (3%)
    pallas_call x1, Pallas kernels, on_device(): pl.pallas_call(functools.partial(kernel, (gx, gy, gz, chunks)), out_shape...  70.1 us
    unnamed x4, local copies, waits for them, and re-layouts  1.85 us

profile of v3, /device:TPU:0, one launch (start us, length us, event | category | flops | bytes accessed | tf_op | source)
XLA Modules:
  0.0 72.6 jit_solution(8495962164242512999)
XLA Ops:
  0.6 70.1 %shard_map.59 = (f32[4,128]{1,0:T(4,128)}, f32[4,4,128]{2,1,0:T(4,128)}) custom-call(bf16[512,256]{1,0:T(8,128)(2,1)} %student.1, bf16[2048,256]{1,0:T(8,128)(2,1)} %teacher.1, s32[4,32]{1,0:T(4,128)} %ids.1, s32[4,32]{1,0:T(4,128)} %valid.1), custom_call_target="tpu_custom_call" | custom-call | tf_op jit(solution)/shard_map/pallas_call | solution.py:273
  70.7 0.0 copy-start
  70.7 1.3 %copy.8 = f32[512]{0:T(512)} copy(f32[512]{0:T(512)} %bitcast.3) | data formatting | bytes 4096
  72.0 0.0 copy-done
  72.0 0.6 copy.9
Async XLA Ops:
  70.7 1.3 %copy-start = (f32[4,4,128]{2,1,0:T(4,128)S(1)}, f32[4,4,128]{2,1,0:T(4,128)}, u32[]{:S(2)}) copy-start(f32[4,4,128]{2,1,0:T(4,128)} %get-tuple-element.5) | copy-start | bytes 24580

commit v4 on v3

--- a/solution.py
+++ b/solution.py
@@ -22,10 +22,10 @@
 
 
 def kernel(
-    sizes, student, teacher, ids, valid, row_out, col_out,
+    sizes, student_far, teacher_far, ids, valid, row_out, col_out,
     stu_stage, stu_buf, tea_stage, tea_buf, kern,
     first_send, first_recv, row_send, row_recv, col_send, col_recv, fin_recv,
-    stu_ss, stu_rs, tea_ss, tea_rs, row_ss, row_rs, col_ss, col_rs,
+    stu_ss, stu_rs, tea_ss, tea_rs, row_ss, row_rs, col_ss, col_rs, student, teacher, load_sem,
 ):
     gx, gy, gz, chunks = sizes
     ix, iy, iz = lax.axis_index("gx"), lax.axis_index("gy"), lax.axis_index("gz")
@@ -70,6 +70,14 @@
     for target in greeted:
         pl.semaphore_signal(barrier, inc=1, device_id=target, device_id_type=MESH)
 
+    loads = [
+        pltpu.make_async_copy(student_far, student, load_sem.at[0]),
+        pltpu.make_async_copy(teacher_far, teacher, load_sem.at[1]),
+    ]
+    for load in loads:
+        load.start()
+    for load in loads:
+        load.wait()
     my_quarter = pl.ds(pl.multiple_of(iy * quarter, 8), quarter)
     stu_stage[...] = student[my_quarter, :].astype(jnp.float32)
     for d in range(1, gz):
@@ -276,7 +284,8 @@
                 jax.ShapeDtypeStruct((row_blocks, TILE), f32),
                 jax.ShapeDtypeStruct((gz, col_blocks, TILE), f32),
             ),
-            in_specs=[pl.BlockSpec(memory_space=pltpu.VMEM)] * 4,
+            in_specs=[pl.BlockSpec(memory_space=pl.ANY)] * 2
+            + [pl.BlockSpec(memory_space=pltpu.VMEM)] * 2,
             out_specs=(pl.BlockSpec(memory_space=pltpu.VMEM),) * 2,
             scratch_shapes=[
                 pltpu.VMEM((rows // gy, width), f32),
@@ -299,6 +308,9 @@
                 dma((ITERS,)),
                 dma((ITERS,)),
                 dma((ITERS,)),
+                pltpu.VMEM(student.shape, student.dtype),
+                pltpu.VMEM(teacher.shape, teacher.dtype),
+                dma((2,)),
             ],
             compiler_params=pltpu.CompilerParams(collective_id=0, has_side_effects=True),
         )(student, teacher, block_ids, block_valid)

time: 72.8 us -> 72.6 us (level)
  no operation moved by 1% of the time
where the time goes in v4:
time: 72.6 us; the launch traced here: 72.4 us
  Pallas kernels  69.9 us (96%)
  local copies, waits for them, and re-layouts  1.85 us (3%)
    pallas_call x1, Pallas kernels, on_device(): pl.pallas_call(functools.partial(kernel, (gx, gy, gz, chunks)), out_shape...  69.9 us
    unnamed x4, local copies, waits for them, and re-layouts  1.85 us

profile of v4, /device:TPU:0, one launch (start us, length us, event | category | flops | bytes accessed | tf_op | source)
XLA Modules:
  0.0 72.4 jit_solution(2376461729862529968)
XLA Ops:
  0.6 69.9 %shard_map.59 = (f32[4,128]{1,0:T(4,128)}, f32[4,4,128]{2,1,0:T(4,128)}) custom-call(bf16[512,256]{1,0:T(8,128)(2,1)} %student_far.1, bf16[2048,256]{1,0:T(8,128)(2,1)} %teacher_far.1, s32[4,32]{1,0:T(4,128)} %ids.1, s32[4,32]{1,0:T(4,128)} %valid.1), custom_call_target="tpu_custom_call" | custom-call | tf_op jit(solution)/shard_map/pallas_call | solution.py:281
  70.5 0.0 copy-start
  70.6 1.3 %copy.8 = f32[512]{0:T(512)} copy(f32[512]{0:T(512)} %bitcast.3) | data formatting | bytes 4096
  71.8 0.0 copy-done
  71.8 0.6 copy.9
Async XLA Ops:
  70.5 1.3 %copy-start = (f32[4,4,128]{2,1,0:T(4,128)S(1)}, f32[4,4,128]{2,1,0:T(4,128)}, u32[]{:S(2)}) copy-start(f32[4,4,128]{2,1,0:T(4,128)} %get-tuple-element.5) | copy-start | bytes 24580
